TPU v7x, 32 devices: a whole 2x2x4 slice. The times are simulated.
32 devices in a mesh: dp: 8 (over z, y), col: 4 (over x, core).
Axes of the slice: x: 2, y: 2, z: 4, core: 2. Of those that a mesh axis runs over, the one named last changes fastest.
Arguments:
- tokens: bfloat16 [8192, 8192], P('dp', 'col'), may hold values from -6 to 6
- out_grad: bfloat16 [8192, 8192], P(('dp', 'col')), may hold values from -6 to 6
- weight: float32 [8192, 8192], P('dp', 'col'), may hold values from -6 to 6
- second: float32 [8192, 8192], P('dp', 'col'), may hold values from 0.0001 to 0.001
- momentum: float32 [8192, 512], P(('dp', 'col')), may hold values from -0.12 to 0.12
- sign_seed: int32 [1], replicated, may hold values from 0 to 999999
- step_number: int32 [1], replicated, may hold values from 1 to 999999
Outputs:
- new_weight: float32 [8192, 8192], P('dp', 'col')
- new_second: float32 [8192, 8192], P('dp', 'col')
- new_momentum: float32 [8192, 512], P(('dp', 'col'))
All inputs are finite; a program needn't handle non-finite values.
Results may differ from a plain program's by a relative error of at most 0.00097.
Values may be sent and summed in bfloat16 or wider, within the bound.
No kernel may reach another device: no remote copies, remote signals or barrier semaphores. Data moves between devices by JAX's collectives and lax.ppermute only.
A program may use at most 128 MiB of HBM per device.

v0:
```python
import jax
import jax.numpy as jnp
from jax import lax
from jax.sharding import PartitionSpec as P


def sign_table(sign_seed, step_number, first_row, row_count, low_rank):
    row_ids = first_row + lax.iota(jnp.int32, row_count)
    col_ids = lax.iota(jnp.int32, low_rank)
    flat_index = row_ids[:, None] * low_rank + col_ids[None, :]
    hashed = flat_index * 747796405 + sign_seed[0] * 1664525 + step_number[0] * 1013904223
    hashed = hashed ^ hashed >> 16 & 65535
    hashed = hashed * 2127912213
    hashed = hashed ^ hashed >> 13 & 524287
    hashed = hashed * 1103515245
    hashed = hashed ^ hashed >> 16 & 65535
    low_bit = hashed >> 20 & 1
    return (1 - 2 * low_bit).astype(jnp.float32)


def contract(left_rows, right_rows):
    return lax.dot_general(
        left_rows, right_rows, (((0,), (0,)), ((), ())), preferred_element_type=jnp.float32
    )


def per_device(tokens, out_grad, weight, second, momentum, sign_seed, step_number):
    local_tokens, din_local = tokens.shape
    low_rank = momentum.shape[1]
    owner_rows = momentum.shape[0]
    inv_root = 1.0 / jnp.sqrt(jnp.float32(low_rank))
    col_position = lax.axis_index("col")
    sign_block = sign_table(sign_seed, step_number, col_position * din_local, din_local, low_rank)
    partial_sketch = (
        jnp.dot(tokens, sign_block.astype(jnp.bfloat16), preferred_element_type=jnp.float32)
        * inv_root
    )
    quarter = lax.psum_scatter(partial_sketch, "col", scatter_dimension=0, tiled=True)
    sketch = quarter.astype(jnp.bfloat16)
    total_tokens = lax.axis_size("dp") * local_tokens
    data_count = lax.axis_size("dp")
    col_count = lax.axis_size("col")
    quarter_rows = out_grad.shape[0]
    grouped = out_grad.reshape(quarter_rows, data_count, col_count, owner_rows)
    grouped = jnp.transpose(grouped, (0, 2, 1, 3)).reshape(
        quarter_rows, col_count, data_count * owner_rows
    )
    regrouped = lax.all_to_all(grouped, "col", split_axis=1, concat_axis=0, tiled=True)
    regrouped = regrouped.reshape(quarter_rows * col_count, data_count * owner_rows)
    shard_sketch = lax.all_gather(sketch, "col", axis=0, tiled=True)
    projected = lax.psum_scatter(
        contract(regrouped, shard_sketch), "dp", scatter_dimension=0, tiled=True
    )
    projected = projected / jnp.float32(total_tokens)
    new_momentum = 0.8 * momentum + 0.2 * projected
    row_block = lax.all_gather(new_momentum, "col", axis=0, tiled=True)
    dense_grad = (
        lax.dot_general(
            row_block,
            sign_block,
            (((1,), (1,)), ((), ())),
            precision=lax.Precision.HIGHEST,
            preferred_element_type=jnp.float32,
        )
        * inv_root
    )
    new_second = 0.95 * second + 0.05 * dense_grad * dense_grad
    new_weight = weight - 0.5 * dense_grad / (jnp.sqrt(new_second) + 1e-08)
    return (new_weight, new_second, new_momentum)


def solution(mesh):
    placed = (
        P("dp", "col"),
        P(("dp", "col"), None),
        P("dp", "col"),
        P("dp", "col"),
        P(("dp", "col"), None),
        P(),
        P(),
    )
    return jax.shard_map(
        per_device,
        mesh=mesh,
        in_specs=placed,
        out_specs=(P("dp", "col"), P("dp", "col"), P(("dp", "col"), None)),
        check_vma=False,
    )
```

profile of v0, /device:TPU:0, one launch (start us, length us, event | category | flops | bytes accessed | tf_op | source)
XLA Modules:
  0.0 263.5 jit_solution(1373859997120523536)
XLA Ops:
  7.2 0.0 reduce-scatter.3.cloned.1.call-start
  8.5 7.7 %multiply_bitcast_fusion = f32[1024,512]{0,1:T(8,128)} fusion(bf16[1024,2048]{1,0:T(8,128)(2,1)} %param.7, s32[]{:T(128)} %bitcast.1, s32[]{:T(128)} %bitcast, s32[2048]{0:T(1024)S(1)} %add_multiply_fusion), kind=kOutput, calls=%fused_computation.9 | convolution fusion | flops 2170028032 | bytes 6299656 | tf_op jit(solution)/shard_map/dot_general | solution.py:35
  16.2 0.0 reduce-scatter.3.cloned.1.call-update
  16.3 7.8 %reshape.26 = bf16[256,8,4,256]{3,2,1,0:T(4,128)(2,1)} reshape(bf16[256,8192]{1,0:T(8,128)(2,1)} %param.8) | data formatting | bytes 8388608 | tf_op jit(solution)/shard_map/reshape | solution.py:44
  24.1 4.9 %copy.16 = bf16[256,8,4,256]{3,1,0,2:T(8,128)(2,1)} copy(bf16[256,8,4,256]{3,2,1,0:T(4,128)(2,1)} %reshape.26) | data formatting | bytes 8388608 | tf_op jit(solution)/shard_map/reshape | solution.py:44
  29.0 7.4 %reshape.27 = bf16[256,4,2048]{2,0,1:T(8,128)(2,1)} reshape(bf16[256,4,8,256]{3,2,0,1:T(8,128)(2,1)} %bitcast.22) | data formatting | bytes 8388608 | tf_op jit(solution)/shard_map/reshape | solution.py:45
  36.3 4.8 %all-to-all-start = ((bf16[256,4,2048]{2,0,1:T(8,128)(2,1)}), bf16[256,4,2048]{2,0,1:T(8,128)(2,1)}, u32[]{:S(2)}, u32[]{:S(2)}) async-start(bf16[256,4,2048]{2,0,1:T(8,128)(2,1)} %reshape.27), calls=%async_computation.1 | async-start | bytes 8388608 | tf_op jit(solution)/shard_map/all_to_all | solution.py:48
  41.2 0.0 all-gather.3.cloned.1.call-start
  41.2 12.6 %reduce-scatter.3.cloned.1.call-done = f32[256,512]{0,1:T(8,128)} async-done(((f32[1024,512]{0,1:T(8,128)}), f32[256,512]{0,1:T(8,128)}) %reduce-scatter.3.cloned.1.call-update) | async-done | bytes 524304 | tf_op jit(solution)/shard_map/reduce_scatter | solution.py:38
  53.8 1.8 convert_element_type.11
  55.6 0.0 all-gather.3.cloned.1.call-update
  55.6 0.0 reduce-scatter.5.cloned.1.call-start
  55.7 44.1 %all-to-all-done = bf16[256,4,2048]{2,0,1:T(8,128)(2,1)} async-done(((bf16[256,4,2048]{2,0,1:T(8,128)(2,1)}), bf16[256,4,2048]{2,0,1:T(8,128)(2,1)}, u32[]{:S(2)}, u32[]{:S(2)}) %all-to-all-start) | async-done | bytes 4194336 | tf_op jit(solution)/shard_map/all_to_all | solution.py:48
  99.7 0.0 all-gather.3.cloned.1.call-done
  99.7 6.9 %convolution_bitcast_fusion = f32[2048,512]{0,1:T(8,128)} fusion(bf16[1024,512]{0,1:T(8,128)(2,1)} %all-gather.3.cloned.1.call-done, bf16[1024,2048]{1,0:T(8,128)(2,1)} %bitcast.6), kind=kOutput, calls=%fused_computation.7 | convolution fusion | flops 2147483648 | bytes 9437184 | tf_op jit(solution)/shard_map/dot_general | solution.py:22
  106.6 0.0 copy-start
  106.6 0.0 reduce-scatter.5.cloned.1.call-update
  106.6 0.2 all-gather.5.cloned.1.call-start
  106.9 0.8 copy-done
  107.6 0.2 copy.12
  107.8 87.7 %reduce-scatter.5.cloned.1.call-done = f32[256,512]{0,1:T(8,128)} async-done(((f32[2048,512]{0,1:T(8,128)}), f32[256,512]{0,1:T(8,128)}) %reduce-scatter.5.cloned.1.call-update) | async-done | bytes 524304 | tf_op jit(solution)/shard_map/reduce_scatter | solution.py:51
  195.5 1.9 multiply_add_fusion.1
  197.5 0.0 all-gather.5.cloned.1.call-update
  197.5 2.0 copy.14
  199.5 20.3 %all-gather.5.cloned.1.call-done = f32[1024,512]{0,1:T(8,128)} async-done(((f32[256,512]{0,1:T(8,128)}), f32[1024,512]{0,1:T(8,128)}) %all-gather.5.cloned.1.call-update) | async-done | bytes 2097168 | tf_op jit(solution)/shard_map/all_gather | solution.py:56
  219.8 37.1 %divide_subtract_fusion = (f32[1024,2048]{1,0:T(8,128)}, f32[1024,2048]{1,0:T(8,128)}) fusion(f32[1024,2048]{1,0:T(8,128)} %param.9, f32[1024,2048]{1,0:T(8,128)} %param.10, f32[1024,512]{0,1:T(8,128)} %all-gather.5.cloned.1.call-done, s32[]{:T(128)} %bitcast.1, s32[]{:T(128)} %bitcast, s32[2048]{0:T(1024)S(1)} %add_multiply_fusion), kind=kOutput, calls=%fused_computation | convolution fusion | flops 12924747776 | bytes 35659784 | tf_op jit(solution)/shard_map/dot_general | solution.py:58
  (1 shorter events, 0.0 us)
Async XLA Ops:
  7.2 46.7 %reduce-scatter.3.cloned.1.call-start = ((), (), s32[]{:S(2)}) async-start(), calls=%async_computation.3 | async-start | bytes 2621440 | tf_op jit(solution)/shard_map/reduce_scatter | solution.py:38
  36.3 63.4 %all-to-all-start = ((bf16[256,4,2048]{2,0,1:T(8,128)(2,1)}), bf16[256,4,2048]{2,0,1:T(8,128)(2,1)}, u32[]{:S(2)}, u32[]{:S(2)}) async-start(bf16[256,4,2048]{2,0,1:T(8,128)(2,1)} %reshape.27), calls=%async_computation.1 | async-start | bytes 8388608 | tf_op jit(solution)/shard_map/all_to_all | solution.py:48
  41.2 58.5 %all-gather.3.cloned.1.call-start = ((), (), s32[]{:S(2)}) async-start(), calls=%async_computation.4 | async-start | bytes 1310720 | tf_op jit(solution)/shard_map/all_gather | solution.py:50
  55.6 139.9 %reduce-scatter.5.cloned.1.call-start = ((), (), s32[]{:S(2)}) async-start(), calls=%async_computation.5 | async-start | bytes 4718592 | tf_op jit(solution)/shard_map/reduce_scatter | solution.py:51
  106.6 1.0 copy-start
  106.6 113.2 %all-gather.5.cloned.1.call-start = ((), (), s32[]{:S(2)}) async-start(), calls=%async_computation.6 | async-start | bytes 2621440 | tf_op jit(solution)/shard_map/all_gather | solution.py:56
Sparse Core Ops, SparseCore 0:
  16.4 37.4 reduce-scatter.2
  56.0 21.9 all-gather.2
  106.7 88.7 reduce-scatter.4
  197.6 22.1 all-gather.4
where the time goes:
time: 264 us; the launch traced here: 263 us
  waiting for transfers between devices  165 us (62%)
  matrix products  51.7 us (20%)
  local copies, waits for them, and re-layouts  23.1 us (9%)
  between operations  15.1 us (6%)
  starting transfers between devices  5.19 us (2%)
  other arithmetic  3.69 us (1%)
    reduce_scatter x1, waiting for transfers between devices, per_device(): lax.psum_scatter(contract(regrouped, shard_sketch), 'dp', scatter_dimensi...  87.7 us
    all_to_all x1, waiting for transfers between devices, per_device(): lax.all_to_all(grouped, 'col', split_axis=1, concat_axis=0, tiled=True)  44.1 us
    dot_general x1, matrix products, per_device(): lax.dot_general(row_block, sign_block, (((1,), (1,)), ((), ())), precisio...  37.1 us
    all_gather x1, waiting for transfers between devices, per_device(): row_block = lax.all_gather(new_momentum, 'col', axis=0, tiled=True)  20.3 us
    reshape x2, local copies, waits for them, and re-layouts, per_device(): grouped = out_grad.reshape(quarter_rows, data_count, col_count, owner_rows)  12.7 us
    reduce_scatter x1, waiting for transfers between devices, per_device(): lax.psum_scatter(partial_sketch, 'col', scatter_dimension=0, tiled=True)  12.6 us
    dot_general x1, matrix products, per_device(): jnp.dot(tokens, sign_block.astype(jnp.bfloat16), preferred_element_type=j...  7.71 us
    reshape x1, local copies, waits for them, and re-layouts, per_device(): jnp.transpose(grouped, (0, 2, 1, 3))  7.37 us
  transfers between devices with their start and end apart: 5, of which 4 were waited for; matrix products, arithmetic and copies ran while one was open for 9% of the time, Pallas kernels for 0%

commit v1 on v0

--- a/solution.py
+++ b/solution.py
@@ -45,7 +45,10 @@
     grouped = jnp.transpose(grouped, (0, 2, 1, 3)).reshape(
         quarter_rows, col_count, data_count * owner_rows
     )
-    regrouped = lax.all_to_all(grouped, "col", split_axis=1, concat_axis=0, tiled=True)
+    regrouped = jnp.concatenate(
+        lax.all_to_all(jnp.stack(jnp.split(grouped, lax.axis_size("col"), axis=1)), "col", 0, 0),
+        axis=0,
+    )
     regrouped = regrouped.reshape(quarter_rows * col_count, data_count * owner_rows)
     shard_sketch = lax.all_gather(sketch, "col", axis=0, tiled=True)
     projected = lax.psum_scatter(

time: 264 us -> 255 us (0.966)
  matrix products: 51.7 us -> 40.2 us
    dot_general x1, matrix products: 37.1 us -> 25.6 us  [per_device(): lax.dot_general(row_block, sign_block, (((1,), (1,)), ((), ())), precisio...]
    reduce_scatter x1, waiting for transfers between devices: 12.6 us -> 4.02 us  [per_device(): lax.psum_scatter(partial_sketch, 'col', scatter_dimension=0, tiled=True)]
    all_to_all x1, waiting for transfers between devices: 44.1 us -> 49 us  [per_device(): lax.all_to_all(jnp.stack(jnp.split(grouped, lax.axis_size('col'), axis=1)...]
    unnamed x4 -> x2, local copies, waits for them, and re-layouts: 3.02 us -> 0.01 us
    another operation x0 -> x1, local copies, waits for them, and re-layouts: none -> 2.75 us  [per_device(): jnp.stack(jnp.split(grouped, lax.axis_size('col'), axis=1))]
  transfers between devices with their start and end apart: 5 -> 5, of which waited for: 4 -> 4; matrix products, arithmetic and copies ran while one was open for 9% -> 11% of each run, Pallas kernels for 0% -> 0%
where the time goes in v1:
time: 255 us; the launch traced here: 254 us
  waiting for transfers between devices  165 us (65%)
  matrix products  40.2 us (16%)
  local copies, waits for them, and re-layouts  22.8 us (9%)
  between operations  15.1 us (6%)
  other arithmetic  6.01 us (2%)
  starting transfers between devices  5.18 us (2%)
    reduce_scatter x1, waiting for transfers between devices, per_device(): lax.psum_scatter(contract(regrouped, shard_sketch), 'dp', scatter_dimensi...  89.2 us
    all_to_all x1, waiting for transfers between devices, per_device(): lax.all_to_all(jnp.stack(jnp.split(grouped, lax.axis_size('col'), axis=1)...  49 us
    dot_general x1, matrix products, per_device(): lax.dot_general(row_block, sign_block, (((1,), (1,)), ((), ())), precisio...  25.6 us
    all_gather x1, waiting for transfers between devices, per_device(): row_block = lax.all_gather(new_momentum, 'col', axis=0, tiled=True)  22.4 us
    reshape x2, local copies, waits for them, and re-layouts, per_device(): grouped = out_grad.reshape(quarter_rows, data_count, col_count, owner_rows)  12.7 us
    dot_general x1, matrix products, per_device(): jnp.dot(tokens, sign_block.astype(jnp.bfloat16), preferred_element_type=j...  7.71 us
    reshape x1, local copies, waits for them, and re-layouts, per_device(): jnp.transpose(grouped, (0, 2, 1, 3))  7.37 us
    dot_general x1, matrix products, contract(): lax.dot_general(left_rows, right_rows, (((0,), (0,)), ((), ())), preferre...  6.9 us
  transfers between devices with their start and end apart: 5, of which 4 were waited for; matrix products, arithmetic and copies ran while one was open for 11% of the time, Pallas kernels for 0%

profile of v1, /device:TPU:0, one launch (start us, length us, event | category | flops | bytes accessed | tf_op | source)
XLA Modules:
  0.0 254.0 jit_solution(12626370248299274747)
XLA Ops:
  7.2 0.0 reduce-scatter.3.cloned.1.call-start
  8.5 7.7 %multiply_bitcast_fusion = f32[1024,512]{0,1:T(8,128)} fusion(bf16[1024,2048]{1,0:T(8,128)(2,1)} %param.7, s32[]{:T(128)} %bitcast.7, s32[]{:T(128)} %bitcast.6, s32[2048]{0:T(1024)S(1)} %add_multiply_fusion), kind=kOutput, calls=%fused_computation.9 | convolution fusion | flops 2170028032 | bytes 6299656 | tf_op jit(solution)/shard_map/dot_general | solution.py:35
  16.2 0.0 reduce-scatter.3.cloned.1.call-update
  16.3 7.8 %reshape.22 = bf16[256,8,4,256]{3,2,1,0:T(4,128)(2,1)} reshape(bf16[256,8192]{1,0:T(8,128)(2,1)} %param.8) | data formatting | bytes 8388608 | tf_op jit(solution)/shard_map/reshape | solution.py:44
  24.1 4.9 %copy.15 = bf16[256,8,4,256]{3,1,0,2:T(8,128)(2,1)} copy(bf16[256,8,4,256]{3,2,1,0:T(4,128)(2,1)} %reshape.22) | data formatting | bytes 8388608 | tf_op jit(solution)/shard_map/reshape | solution.py:44
  29.0 7.4 %reshape.23 = bf16[256,4,2048]{2,0,1:T(8,128)(2,1)} reshape(bf16[256,4,8,256]{3,2,0,1:T(8,128)(2,1)} %bitcast.24) | data formatting | bytes 8388608 | tf_op jit(solution)/shard_map/reshape | solution.py:45
  36.3 2.7 %slice_bitcast_fusion.3 = (bf16[1,256,1,2048]{3,1,2,0:T(8,128)(2,1)S(1)}, bf16[1,256,1,2048]{3,1,2,0:T(8,128)(2,1)S(1)}, bf16[1,256,1,2048]{3,1,2,0:T(8,128)(2,1)S(1)}, bf16[1,256,1,2048]{3,1,2,0:T(8,128)(2,1)S(1)}) fusion(bf16[256,4,2048]{2,0,1:T(8,128)(2,1)} %reshape.23), kind=kLoop, calls=%fused_computation.13 | loop fusion | bytes 8388608 | tf_op jit(solution)/shard_map/stack | solution.py:49
  39.1 2.3 pad_maximum_fusion
  41.4 4.8 %all-to-all-start = ((bf16[4,256,1,2048]{3,1,2,0:T(8,128)(2,1)}), bf16[4,256,1,2048]{3,1,2,0:T(8,128)(2,1)}, u32[]{:S(2)}, u32[]{:S(2)}) async-start(bf16[4,256,1,2048]{3,1,2,0:T(8,128)(2,1)} %pad_maximum_fusion), calls=%async_computation | async-start | bytes 8388608 | tf_op jit(solution)/shard_map/all_to_all | solution.py:49
  46.2 0.0 all-gather.3.cloned.1.call-start
  46.3 4.0 %reduce-scatter.3.cloned.1.call-done = f32[256,512]{0,1:T(8,128)} async-done(((f32[1024,512]{0,1:T(8,128)}), f32[256,512]{0,1:T(8,128)}) %reduce-scatter.3.cloned.1.call-update) | async-done | bytes 524304 | tf_op jit(solution)/shard_map/reduce_scatter | solution.py:38
  50.3 1.8 convert_element_type.11
  52.1 0.0 all-gather.3.cloned.1.call-update
  52.1 0.0 reduce-scatter.5.cloned.1.call-start
  52.1 49.0 %all-to-all-done = bf16[4,256,1,2048]{3,1,2,0:T(8,128)(2,1)} async-done(((bf16[4,256,1,2048]{3,1,2,0:T(8,128)(2,1)}), bf16[4,256,1,2048]{3,1,2,0:T(8,128)(2,1)}, u32[]{:S(2)}, u32[]{:S(2)}) %all-to-all-start) | async-done | bytes 4194336 | tf_op jit(solution)/shard_map/all_to_all | solution.py:49
  101.2 0.0 all-gather.3.cloned.1.call-done
  101.2 6.9 %fusion.23 = f32[2048,512]{1,0:T(8,128)} fusion(bf16[1024,2048]{1,0:T(8,128)(2,1)} %bitcast.5, bf16[1024,512]{0,1:T(8,128)(2,1)} %all-gather.3.cloned.1.call-done), kind=kOutput, calls=%fused_computation.36 | convolution fusion | flops 2147483648 | bytes 9437184 | tf_op jit(solution)/shard_map/dot_general | solution.py:22
  108.1 0.0 copy-start
  108.1 0.0 reduce-scatter.5.cloned.1.call-update
  108.1 0.2 all-gather.5.cloned.1.call-start
  108.3 89.2 %reduce-scatter.5.cloned.1.call-done = f32[256,512]{1,0:T(8,128)} async-done(((f32[2048,512]{1,0:T(8,128)}), f32[256,512]{1,0:T(8,128)}) %reduce-scatter.5.cloned.1.call-update) | async-done | bytes 524304 | tf_op jit(solution)/shard_map/reduce_scatter | solution.py:54
  197.6 0.0 copy-done
  197.6 1.9 multiply_add_fusion.1
  199.5 0.0 all-gather.5.cloned.1.call-update
  199.5 22.4 %all-gather.5.cloned.1.call-done = f32[1024,512]{1,0:T(8,128)} async-done(((f32[256,512]{1,0:T(8,128)}), f32[1024,512]{1,0:T(8,128)}) %all-gather.5.cloned.1.call-update) | async-done | bytes 2097168 | tf_op jit(solution)/shard_map/all_gather | solution.py:59
  221.9 25.6 %divide_subtract_fusion = (f32[1024,2048]{1,0:T(8,128)}, f32[1024,2048]{1,0:T(8,128)}) fusion(f32[1024,2048]{1,0:T(8,128)} %param.9, f32[1024,2048]{1,0:T(8,128)} %param.10, f32[1024,512]{1,0:T(8,128)} %all-gather.5.cloned.1.call-done, s32[]{:T(128)} %bitcast.7, s32[]{:T(128)} %bitcast.6, s32[2048]{0:T(1024)S(1)} %add_multiply_fusion), kind=kOutput, calls=%fused_computation | convolution fusion | flops 12924747776 | bytes 35659784 | tf_op jit(solution)/shard_map/dot_general | solution.py:61
  (1 shorter events, 0.0 us)
Async XLA Ops:
  7.2 43.1 %reduce-scatter.3.cloned.1.call-start = ((), (), s32[]{:S(2)}) async-start(), calls=%async_computation.3 | async-start | bytes 2621440 | tf_op jit(solution)/shard_map/reduce_scatter | solution.py:38
  41.4 59.8 %all-to-all-start = ((bf16[4,256,1,2048]{3,1,2,0:T(8,128)(2,1)}), bf16[4,256,1,2048]{3,1,2,0:T(8,128)(2,1)}, u32[]{:S(2)}, u32[]{:S(2)}) async-start(bf16[4,256,1,2048]{3,1,2,0:T(8,128)(2,1)} %pad_maximum_fusion), calls=%async_computation | async-start | bytes 8388608 | tf_op jit(solution)/shard_map/all_to_all | solution.py:49
  46.2 55.0 %all-gather.3.cloned.1.call-start = ((), (), s32[]{:S(2)}) async-start(), calls=%async_computation.4 | async-start | bytes 1310720 | tf_op jit(solution)/shard_map/all_gather | solution.py:53
  52.1 145.5 %reduce-scatter.5.cloned.1.call-start = ((), (), s32[]{:S(2)}) async-start(), calls=%async_computation.5 | async-start | bytes 4718592 | tf_op jit(solution)/shard_map/reduce_scatter | solution.py:54
  108.1 89.5 %copy-start = (f32[256,512]{1,0:T(8,128)S(1)}, f32[256,512]{1,0:T(8,128)}, u32[]{:S(2)}) copy-start(f32[256,512]{1,0:T(8,128)} %param.11) | copy-start | bytes 1572868
  108.1 113.8 %all-gather.5.cloned.1.call-start = ((), (), s32[]{:S(2)}) async-start(), calls=%async_computation.6 | async-start | bytes 2621440 | tf_op jit(solution)/shard_map/all_gather | solution.py:59
Sparse Core Ops, SparseCore 0:
  16.4 33.8 reduce-scatter.2
  52.4 22.7 all-gather.2
  108.2 89.2 reduce-scatter.4
  199.6 22.1 all-gather.4
